TPU v7x, 256 devices: a whole 4x4x8 slice. The times are simulated.
256 devices in a mesh: ctx: 16 (over y, x), tp: 16 (over z, core).
Axes of the slice: x: 4, y: 4, z: 8, core: 2. Of those that a mesh axis runs over, the one named last changes fastest.
Arguments:
- residual: bfloat16 [2048, 6144], P('ctx', 'tp'), may hold values from -65 to 65
- query_rows: bfloat16 [2048, 8192], P('ctx', 'tp'), may hold values from -6 to 6
- key_rows: bfloat16 [2048, 8192], P('ctx', 'tp'), may hold values from -6 to 6
- value_rows: bfloat16 [2048, 8192], P('ctx', 'tp'), may hold values from -6 to 6
- head_rates: float32 [64], replicated, may hold values from 0 to 1
- doc_lengths: int32 [4], replicated, may hold values from 1 to 1024, 2048 in all
- attn_gain: float32 [8192], P('tp'), may hold values from 0.1 to 1.9
- out_weight: bfloat16 [8192, 6144], P('tp', 'ctx'), may hold values from -0.09375 to 0.09375
- moe_gain: float32 [6144], P('tp'), may hold values from 0.1 to 1.9
- expert_ids: int32 [2048, 2], P('ctx'), may hold values from 0 to 15, all different within a row; in each aligned block of 128 rows (0 to 127, 128 to 255, ...) at most 24 rows name the same one
- expert_weights: float32 [2048, 2], P('ctx'), may hold values from 0.2 to 1
- gate_weight: bfloat16 [16, 6144, 4608], P('ctx', None, 'tp'), may hold values from -0.078125 to 0.078125
- up_weight: bfloat16 [16, 6144, 4608], P('ctx', None, 'tp'), may hold values from -0.078125 to 0.078125
- down_weight: bfloat16 [16, 4608, 6144], P('ctx', 'tp'), may hold values from -0.125 to 0.125
Outputs:
- output: bfloat16 [2048, 6144], P('ctx', 'tp')
Inputs may be any that keep to these rules, and one draw needn't show every extreme that they name: `expert_ids`: each token names 2 different experts; among the tokens of one device (aligned blocks of 128 rows) no expert is named more than 24 times, a bound that some block reaches. `doc_lengths`: the longest document holds exactly 1024 positions.
All inputs are finite; a program needn't handle non-finite values.
Results may differ from a plain program's by a relative error of at most 0.015.
Values may be sent and summed in bfloat16 or wider, within the bound.
A program may use at most 64 MiB of HBM per device.

v0:
```python
import jax
import jax.numpy as jnp
from jax import lax
from jax.sharding import Mesh
from jax.sharding import PartitionSpec as P

D = 6144
HD = 128
TOP = 2
CTX = ("ctx_0", "ctx_1")
TP = ("tp_0", "tp_1")


def nothing_yet(x, identity):
    return jax.tree.map(
        lambda part, zero: jnp.zeros_like(part) + jnp.asarray(zero, part.dtype), x, identity
    )


def carried_in(x, axes, combine, identity):
    before = start = nothing_yet(x, identity)
    running = x
    for axis in reversed(axes):
        peers, index = (lax.axis_size(axis), lax.axis_index(axis))
        pieces = jax.tree.map(
            lambda part, kind: lax.all_gather(part.astype(kind), axis),
            running,
            (jnp.bfloat16, jnp.bfloat16),
        )
        inside, running = (start, start)
        for k in range(peers):
            passed = k < index
            running = combine(
                running, jax.tree.map(lambda part, own: part[k].astype(own.dtype), pieces, x)
            )
            inside = jax.tree.map(lambda new, old: jnp.where(passed, new, old), running, inside)
        before = combine(inside, before)
    return before


def cut_along(x, dim, peers):
    lengths = x.shape
    tiles = x.reshape(*lengths[:dim], peers, lengths[dim] // peers, *lengths[dim + 1 :])
    return jnp.moveaxis(tiles, dim, 0)


def sum_at_owner(x, axis, dim):
    peers = lax.axis_size(axis)
    tiles = lax.all_to_all(cut_along(x, dim, peers), axis, 0, 0, tiled=True)
    return jnp.sum(tiles.astype(jnp.float32), axis=0)


def sent_to_all(x, axis):
    peers = lax.axis_size(axis)
    return lax.all_to_all(jnp.broadcast_to(x[None], (peers, *x.shape)), axis, 0, 0, tiled=True)


def taken_together(x, axis):
    return sent_to_all(x, axis).sum(axis=0)


def summed_rows(x, chips, core, dim):
    sizes = (lax.axis_size(chips), lax.axis_size(core))
    tiles = cut_along(x, dim, sizes[0] * sizes[1])
    inside = tiles.shape[1:]
    tiles = tiles.reshape(*sizes, *inside).swapaxes(0, 1).reshape(-1, *inside)
    tiles = lax.psum_scatter(tiles, core, scatter_dimension=0, tiled=True)
    return lax.psum_scatter(tiles, chips, scatter_dimension=0, tiled=True)[0]


def segment_of(doc_lengths, positions):
    doc_ends = jnp.cumsum(doc_lengths)
    doc_starts = doc_ends - doc_lengths
    return jnp.sum((positions[:, None] >= doc_starts[None, :]).astype(jnp.int32), axis=1) - 1


def local_attention(query_h, key_h, value_h, head_decay, segments, seg_before):
    length = query_h.shape[0]
    offsets = jnp.arange(length, dtype=jnp.int32)
    distance = (offsets[:, None] - offsets[None, :]).astype(jnp.float32)
    allowed = (offsets[:, None] >= offsets[None, :]) & (segments[:, None] == segments[None, :])
    decay_mask = jnp.where(
        allowed[None], jnp.exp(-head_decay[:, None, None] * jnp.maximum(distance, 0.0)[None]), 0.0
    )
    scores = jnp.einsum("ihd,jhd->hij", query_h, key_h, preferred_element_type=jnp.float32)
    weights = (scores * decay_mask).astype(jnp.bfloat16)
    within = jnp.einsum("hij,jhd->ihd", weights, value_h, preferred_element_type=jnp.float32)
    last_seg = segments[length - 1]
    fading = jnp.where(
        (segments == last_seg)[:, None],
        jnp.exp(-head_decay[None, :] * (length - 1 - offsets).astype(jnp.float32)[:, None]),
        0.0,
    )
    weighted_keys = key_h.astype(jnp.float32) * fading[:, :, None]
    local_state = jnp.einsum(
        "jhd,jhe->hde", weighted_keys, value_h.astype(jnp.float32), precision=lax.Precision.HIGHEST
    )
    carry_factor = jnp.where(last_seg == seg_before, jnp.exp(-head_decay * length), 0.0)
    reaching = jnp.where(
        (segments == seg_before)[:, None],
        jnp.exp(-head_decay[None, :] * (offsets + 1).astype(jnp.float32)[:, None]),
        0.0,
    )
    return (within, local_state, carry_factor, reaching)


def shards(
    residual,
    query_rows,
    key_rows,
    value_rows,
    head_rates,
    doc_lengths,
    attn_gain,
    out_weight,
    moe_gain,
    expert_ids,
    expert_weights,
    gate_weight,
    up_weight,
    down_weight,
):
    length = query_rows.shape[0]
    local_heads = attn_gain.shape[0] // HD
    ctx_index = lax.axis_index(CTX)
    tp_index = lax.axis_index(TP)
    head_decay = lax.dynamic_slice_in_dim(head_rates, tp_index * local_heads, local_heads)
    first_pos = ctx_index * length
    positions = first_pos + jnp.arange(length, dtype=jnp.int32)
    segments = segment_of(doc_lengths, positions)
    seg_before = segment_of(doc_lengths, jnp.reshape(first_pos - 1, (1,)))[0]
    query_h = query_rows.reshape(length, local_heads, HD)
    key_h = key_rows.reshape(length, local_heads, HD)
    value_h = value_rows.reshape(length, local_heads, HD)
    within, local_state, carry_factor, reaching = local_attention(
        query_h, key_h, value_h, head_decay, segments, seg_before
    )

    def combine(earlier, later_one):
        return (earlier[0] * later_one[0], later_one[0][:, None, None] * earlier[1] + later_one[1])

    prefix = carried_in(
        (carry_factor, local_state),
        CTX,
        combine,
        (jnp.ones_like(carry_factor), jnp.zeros_like(local_state)),
    )
    incoming = prefix[1]
    inter = (
        jnp.einsum(
            "ihd,hde->ihe", query_h.astype(jnp.float32), incoming, precision=lax.Precision.HIGHEST
        )
        * reaching[:, :, None]
    )
    mixed_out = within + inter
    scaled = mixed_out * lax.rsqrt(jnp.mean(mixed_out * mixed_out, axis=-1, keepdims=True) + 1e-06)
    heads_out = (scaled.reshape(length, local_heads * HD) * attn_gain).astype(jnp.bfloat16)
    partial_out = jnp.dot(
        heads_out,
        lax.all_gather(out_weight, CTX, axis=1, tiled=True),
        preferred_element_type=jnp.float32,
    )
    attn_out = sum_at_owner(partial_out.astype(jnp.bfloat16), TP, 1)
    hidden_state = (residual.astype(jnp.float32) + attn_out).astype(jnp.bfloat16)
    widened = hidden_state.astype(jnp.float32)
    sum_squares = taken_together(jnp.sum(widened * widened, axis=1), TP)
    moe_input = (widened * lax.rsqrt(sum_squares / D + 1e-05)[:, None] * moe_gain).astype(
        jnp.bfloat16
    )
    experts = lax.axis_size(CTX)
    capacity = 3 * length * TOP // (2 * experts)
    flat_ids = expert_ids.reshape(-1)
    onehot = (flat_ids[:, None] == jnp.arange(experts, dtype=jnp.int32)[None, :]).astype(jnp.int32)
    slot_ranks = jnp.sum((jnp.cumsum(onehot, axis=0) - onehot) * onehot, axis=1)
    slot_index = flat_ids * capacity + slot_ranks
    source_row = (
        jnp.zeros((experts * capacity,), jnp.int32)
        .at[slot_index]
        .set(jnp.arange(length * TOP, dtype=jnp.int32) // TOP)
    )
    occupied = jnp.zeros((experts * capacity,), jnp.bool_).at[slot_index].set(True)
    picked_rows = jnp.where(
        occupied[:, None], moe_input[source_row], jnp.zeros((), moe_input.dtype)
    )
    arrived = lax.all_gather(
        lax.all_to_all(
            picked_rows.reshape(experts, capacity, moe_input.shape[1]),
            CTX,
            split_axis=0,
            concat_axis=0,
            tiled=True,
        ),
        TP,
        axis=2,
        tiled=True,
    )
    flat_in = arrived.reshape(-1, arrived.shape[2])
    gate_pre = jnp.dot(flat_in, gate_weight[0], preferred_element_type=jnp.float32)
    up_pre = jnp.dot(flat_in, up_weight[0], preferred_element_type=jnp.float32)
    activated = (jax.nn.silu(gate_pre) * up_pre).astype(jnp.bfloat16)
    down_term = jnp.dot(activated, down_weight[0], preferred_element_type=jnp.float32)
    reduced = summed_rows(down_term.astype(jnp.bfloat16), "tp_0", "tp_1", 1).astype(jnp.float32)
    outbound = reduced.astype(jnp.bfloat16).reshape(
        arrived.shape[0], arrived.shape[1], reduced.shape[1]
    )
    returned = lax.all_to_all(outbound, CTX, split_axis=0, concat_axis=0, tiled=True)
    returned_flat = returned.reshape(experts * capacity, returned.shape[2])
    gathered_out = (
        returned_flat[slot_index].reshape(length, TOP, returned.shape[2]).astype(jnp.float32)
    )
    mixture = jnp.sum(gathered_out * expert_weights[:, :, None], axis=1)
    return (widened + mixture).astype(jnp.bfloat16)


def solution(mesh):
    finer = Mesh(mesh.devices.reshape(4, 4, 8, 2), ("ctx_0", "ctx_1", "tp_0", "tp_1"))
    placed = (
        P(CTX, TP),
        P(CTX, TP),
        P(CTX, TP),
        P(CTX, TP),
        P(),
        P(),
        P(TP),
        P(TP, CTX),
        P(TP),
        P(CTX, None),
        P(CTX, None),
        P(CTX, None, TP),
        P(CTX, None, TP),
        P(CTX, TP, None),
    )
    return jax.shard_map(shards, mesh=finer, in_specs=placed, out_specs=P(CTX, TP), check_vma=False)
```

profile of v0, /device:TPU:2, one launch (start us, length us, event | category | flops | bytes accessed | tf_op | source)
XLA Modules:
  0.0 320.3 jit_solution(3398791720834157552)
XLA Ops:
  6.5 0.7 all-gather.6.cloned.1.call-update
  7.3 1.1 reduce-window.19
  8.4 1.3 fusion.98
  12.2 1.3 dynamic-slice
  14.2 0.7 fusion.97
  15.1 9.9 %all-reduce = bf16[16]{0:T(256)(128)(2,1)S(1)} all-reduce(bf16[16]{0:T(256)(128)(2,1)S(1)} %dynamic-update-slice), channel_id=2, replica_groups=mesh['ctx_0'=4,'ctx_1'=4,'tp_0'=8,'tp_1'=2] {'ctx_1'}, use_global_device_ids=true, to_apply=%add | all-reduce | flops 16 | bytes 64
  25.1 0.6 broadcast_select_fusion.5
  25.7 8.6 %all-gather.2 = bf16[4,1,4]{2,1,0:T(2,128)(2,1)S(1)} all-gather(bf16[1,1,4]{2,1,0:T(2,128)(2,1)S(1)} %bitcast.205), channel_id=1, replica_groups=mesh['ctx_0'=4,'ctx_1'=4,'tp_0'=8,'tp_1'=2] {'ctx_0'}, dimensions={0}, use_global_device_ids=true | all-gather | bytes 40 | tf_op jit(solution)/shard_map/all_gather | solution.py:26
  34.3 1.7 copy.92
  36.0 0.6 convert_maximum_fusion
  36.6 1.3 broadcast_compare_fusion
  37.9 0.7 exponential_select_fusion
  38.6 1.2 convolution_convert_fusion.2
  39.8 12.2 %all-gather.1 = bf16[16,128,128]{2,1,0:T(8,128)(2,1)S(1)} all-gather(bf16[4,128,128]{2,1,0:T(8,128)(2,1)S(1)} %convolution_convert_fusion.2), channel_id=3, replica_groups=mesh['ctx_0'=4,'ctx_1'=4,'tp_0'=8,'tp_1'=2] {'ctx_1'}, dimensions={0}, use_global_device_ids=true | all-gather | bytes 655360 | tf_op jit(solution)/shard_map/all_gather | solution.py:26
  52.1 0.7 copy-done.1
  53.0 15.7 %all_gather.31 = bf16[4,4,128,128]{3,2,1,0:T(8,128)(2,1)} all-gather(bf16[1,4,128,128]{3,2,1,0:T(8,128)(2,1)S(1)} %fusion.28), channel_id=1, replica_groups=mesh['ctx_0'=4,'ctx_1'=4,'tp_0'=8,'tp_1'=2] {'ctx_0'}, dimensions={0}, use_global_device_ids=true | all-gather | bytes 655360 | tf_op jit(solution)/shard_map/all_gather | solution.py:26
  69.9 0.8 fusion.88
  70.7 2.1 convolution_bitcast_fusion.1
  72.9 2.1 multiply_reduce_fusion.1
  75.1 0.8 fusion.37
  75.8 10.6 %all-gather.6.cloned.1.call-done = bf16[512,6144]{1,0:T(8,128)(2,1)} async-done(((bf16[512,384]{1,0:T(8,128)(2,1)}), bf16[512,6144]{1,0:T(8,128)(2,1)}) %all-gather.6.cloned.1.call-update) | async-done | bytes 6291472 | tf_op jit(solution)/shard_map/all_gather | solution.py:160
  86.4 3.9 %convolution_convert_fusion.1 = bf16[128,6144]{1,0:T(8,128)(2,1)S(1)} fusion(bf16[128,512]{0,1:T(8,128)(2,1)} %fusion.37, bf16[512,6144]{1,0:T(8,128)(2,1)} %all-gather.6.cloned.1.call-done), kind=kOutput, calls=%fused_computation.5 | convolution fusion | flops 806092800 | bytes 7995392 | tf_op jit(solution)/shard_map/dot_general | solution.py:158
  90.4 1.4 copy.121
  91.7 7.7 %all-to-all-start = ((bf16[16,128,384]{2,1,0:T(8,128)(2,1)}), bf16[16,128,384]{2,1,0:T(8,128)(2,1)}, u32[]{:S(2)}, u32[]{:S(2)}) async-start(bf16[16,128,384]{2,1,0:T(8,128)(2,1)} %bitcast.194), calls=%async_computation | async-start | bytes 3145728 | tf_op jit(solution)/shard_map/all_to_all | solution.py:49
  99.5 0.7 copy.84
  100.2 1.0 eq.77
  101.2 1.6 eq.73
  103.4 1.3 reduce-window.20
  104.7 0.7 slice_reduce_fusion
  105.4 1.2 reduce-window.21
  106.6 1.2 slice.75
  107.8 1.3 broadcast_multiply_fusion.1
  109.1 1.4 copy.83
  110.5 1.6 mul.332
  112.6 0.8 fusion.91
  113.4 0.7 compare_select_fusion
  114.1 1.6 scatter_custom_fusion.1
  115.7 21.7 %all-to-all-done = bf16[16,128,384]{2,1,0:T(8,128)(2,1)} async-done(((bf16[16,128,384]{2,1,0:T(8,128)(2,1)}), bf16[16,128,384]{2,1,0:T(8,128)(2,1)}, u32[]{:S(2)}, u32[]{:S(2)}) %all-to-all-start) | async-done | bytes 1572896 | tf_op jit(solution)/shard_map/all_to_all | solution.py:49
  137.4 1.6 convert_reduce_fusion
  139.0 1.6 fusion.47
  141.2 4.8 %all-to-all-start.1 = ((f32[16,1,128]{2,1,0:T(1,128)}), f32[16,1,128]{2,1,0:T(1,128)S(1)}, u32[]{:S(2)}, u32[]{:S(2)}) async-start(f32[16,1,128]{2,1,0:T(1,128)} %broadcast_in_dim.65), calls=%async_computation.1 | async-start | bytes 16384 | tf_op jit(solution)/shard_map/all_to_all | solution.py:55
  146.1 2.1 scatter_custom_fusion
  148.2 0.7 broadcast_in_dim.63
  148.9 4.7 %all-to-all-done.1 = f32[16,1,128]{2,1,0:T(1,128)S(1)} async-done(((f32[16,1,128]{2,1,0:T(1,128)}), f32[16,1,128]{2,1,0:T(1,128)S(1)}, u32[]{:S(2)}, u32[]{:S(2)}) %all-to-all-start.1) | async-done | bytes 8224 | tf_op jit(solution)/shard_map/all_to_all | solution.py:55
  154.2 0.7 add_rsqrt_fusion.1
  154.9 1.6 fusion.49
  156.5 3.3 %gather_fusion = bf16[384,384]{1,0:T(8,128)(2,1)} fusion(bf16[128,384]{1,0:T(8,128)(2,1)} %fusion.49, s32[1024]{0:T(1024)S(1)} %pad_clamp_fusion.1), kind=kCustom, calls=%fused_computation | custom fusion | bytes 591360 | tf_op jit(solution)/shard_map/gather | solution.py:183
  159.9 1.1 broadcast_select_fusion
  160.9 14.6 %all_to_all.21 = bf16[16,24,384]{2,1,0:T(8,128)(2,1)} all-to-all(bf16[16,24,384]{2,1,0:T(8,128)(2,1)S(1)} %broadcast_select_fusion), channel_id=1, replica_groups=mesh['ctx_0'=4,'ctx_1'=4,'tp_0'=8,'tp_1'=2] {'ctx_0','ctx_1'}, dimensions={0} | all-to-all | bytes 589824 | tf_op jit(solution)/shard_map/all_to_all | solution.py:186
  175.8 37.1 %all-gather.8.cloned.1.call-done = bf16[16,24,6144]{2,1,0:T(8,128)(2,1)} async-done(((bf16[16,24,384]{2,1,0:T(8,128)(2,1)}), bf16[16,24,6144]{2,1,0:T(8,128)(2,1)}) %all-gather.8.cloned.1.call-update) | async-done | bytes 4718608 | tf_op jit(solution)/shard_map/all_gather | solution.py:185
  213.0 5.6 %fusion.3 = f32[384,288]{0,1:T(8,128)S(1)} fusion(bf16[384,6144]{1,0:T(8,128)(2,1)} %bitcast.207, bf16[1,6144,288]{1,2,0:T(8,128)(2,1)} %param.25), kind=kOutput, calls=%fused_computation.10 | convolution fusion | flops 1358954496 | bytes 8699904 | tf_op jit(solution)/shard_map/dot_general | solution.py:198
  218.8 2.0 fusion.8
  220.8 2.9 convolution_convert_fusion
  223.7 0.7 copy.120
  224.4 2.7 copy.89
  227.2 16.7 %reduce-scatter.3.cloned.1.call-done = bf16[8,384,384]{2,1,0:T(8,128)(2,1)} async-done(((bf16[16,384,384]{2,1,0:T(8,128)(2,1)}), bf16[8,384,384]{2,1,0:T(8,128)(2,1)}) %reduce-scatter.3.cloned.1.call-update) | async-done | bytes 2359312 | tf_op jit(solution)/shard_map/reduce_scatter | solution.py:67
  243.9 47.2 %reduce-scatter.5.cloned.1.call-done = bf16[1,384,384]{2,1,0:T(8,128)(2,1)} async-done(((bf16[8,384,384]{2,1,0:T(8,128)(2,1)}), bf16[1,384,384]{2,1,0:T(8,128)(2,1)}) %reduce-scatter.5.cloned.1.call-update) | async-done | bytes 294928 | tf_op jit(solution)/shard_map/reduce_scatter | solution.py:68
  291.1 7.3 %all-to-all-start.3 = ((bf16[16,24,384]{2,1,0:T(8,128)(2,1)}), bf16[16,24,384]{2,1,0:T(8,128)(2,1)}, u32[]{:S(2)}, u32[]{:S(2)}) async-start(bf16[16,24,384]{2,1,0:T(8,128)(2,1)} %bitcast.199), calls=%async_computation.5 | async-start | bytes 589824 | tf_op jit(solution)/shard_map/all_to_all | solution.py:206
  298.4 0.7 copy.90
  299.2 6.9 %all-to-all-done.3 = bf16[16,24,384]{2,1,0:T(8,128)(2,1)} async-done(((bf16[16,24,384]{2,1,0:T(8,128)(2,1)}), bf16[16,24,384]{2,1,0:T(8,128)(2,1)}, u32[]{:S(2)}, u32[]{:S(2)}) %all-to-all-start.3) | async-done | bytes 294944 | tf_op jit(solution)/shard_map/all_to_all | solution.py:206
  306.0 2.8 gather_fusion.1
  308.8 1.9 reshape.435
  310.7 1.5 multiply_reduce_fusion
  312.2 1.6 fusion.50
  (59 shorter events, 6.0 us)
Async XLA Ops:
  6.5 214.3 %copy-start = (bf16[1,288,6144]{2,1,0:T(8,128)(2,1)S(1)}, bf16[1,288,6144]{2,1,0:T(8,128)(2,1)}, u32[]{:S(2)}) copy-start(bf16[1,288,6144]{2,1,0:T(8,128)(2,1)} %param.27) | copy-start | bytes 10616836
  6.5 79.9 %all-gather.6.cloned.1.call-start = ((), (), s32[]{:S(2)}) async-start(), calls=%async_computation.6 | async-start | bytes 6684672 | tf_op jit(solution)/shard_map/all_gather | solution.py:160
  9.8 1.2 copy-start.13
  9.8 0.6 copy-start.10
  14.9 54.4 %copy-start.11 = (f32[4]{0:T(128)}, f32[4]{0:T(128)S(1)}, u32[]{:S(2)}) copy-start(f32[4]{0:T(128)S(1)} %get-tuple-element.10) | copy-start | bytes 52
  25.7 43.6 %copy-start.9 = (f32[4]{0:T(128)}, f32[4]{0:T(128)S(1)}, u32[]{:S(2)}) copy-start(f32[4]{0:T(128)S(1)} %get-tuple-element.16) | copy-start | bytes 52
  52.0 0.8 copy-start.1
  52.1 17.8 %copy-start.6 = (f32[4]{0:T(128)}, f32[4]{0:T(128)S(1)}, u32[]{:S(2)}) copy-start(f32[4]{0:T(128)S(1)} %get-tuple-element.21) | copy-start | bytes 52
  52.1 17.8 %copy-start.7 = (f32[4]{0:T(128)}, f32[4]{0:T(128)S(1)}, u32[]{:S(2)}) copy-start(f32[4]{0:T(128)S(1)} %get-tuple-element.22) | copy-start | bytes 52
  52.1 17.8 %copy-start.8 = (f32[4]{0:T(128)}, f32[4]{0:T(128)S(1)}, u32[]{:S(2)}) copy-start(f32[4]{0:T(128)S(1)} %get-tuple-element.23) | copy-start | bytes 52
  72.9 2.2 copy-start.5
  90.3 9.2 %copy-start.2 = (s32[128,2]{0,1:T(2,128)S(1)}, s32[128,2]{0,1:T(2,128)}, u32[]{:S(2)}) copy-start(s32[128,2]{0,1:T(2,128)} %param.23) | copy-start | bytes 3076
  91.7 45.7 %all-to-all-start = ((bf16[16,128,384]{2,1,0:T(8,128)(2,1)}), bf16[16,128,384]{2,1,0:T(8,128)(2,1)}, u32[]{:S(2)}, u32[]{:S(2)}) async-start(bf16[16,128,384]{2,1,0:T(8,128)(2,1)} %bitcast.194), calls=%async_computation | async-start | bytes 3145728 | tf_op jit(solution)/shard_map/all_to_all | solution.py:49
  114.1 27.1 %copy-start.3 = (s32[256,1]{0,1:T(1,128)}, s32[256,1]{0,1:T(1,128)S(1)}, u32[]{:S(2)}) copy-start(s32[256,1]{0,1:T(1,128)S(1)} %compare_select_fusion) | copy-start | bytes 3076
  141.2 12.4 %all-to-all-start.1 = ((f32[16,1,128]{2,1,0:T(1,128)}), f32[16,1,128]{2,1,0:T(1,128)S(1)}, u32[]{:S(2)}, u32[]{:S(2)}) async-start(f32[16,1,128]{2,1,0:T(1,128)} %broadcast_in_dim.65), calls=%async_computation.1 | async-start | bytes 16384 | tf_op jit(solution)/shard_map/all_to_all | solution.py:55
  146.0 66.9 %all-gather.8.cloned.1.call-start = ((), (), s32[]{:S(2)}) async-start(), calls=%async_computation.7 | async-start | bytes 5013504 | tf_op jit(solution)/shard_map/all_gather | solution.py:185
  175.6 68.3 %reduce-scatter.3.cloned.1.call-start = ((), (), s32[]{:S(2)}) async-start(), calls=%async_computation.8 | async-start | bytes 7077888 | tf_op jit(solution)/shard_map/reduce_scatter | solution.py:67
  213.0 5.6 %copy-start.14 = (bf16[16,24,6144]{2,1,0:T(8,128)(2,1)S(1)}, bf16[16,24,6144]{2,1,0:T(8,128)(2,1)}, u32[]{:S(2)}) copy-start(bf16[16,24,6144]{2,1,0:T(8,128)(2,1)} %all-gather.8.cloned.1.call-done) | copy-start | bytes 14155780
  213.0 5.9 %copy-start.15 = (bf16[1,6144,288]{1,2,0:T(8,128)(2,1)S(1)}, bf16[1,6144,288]{1,2,0:T(8,128)(2,1)}, u32[]{:S(2)}) copy-start(bf16[1,6144,288]{1,2,0:T(8,128)(2,1)} %param.26) | copy-start | bytes 10616836
  227.1 71.3 %copy-start.12 = (f32[128,2]{0,1:T(2,128)S(1)}, f32[128,2]{0,1:T(2,128)}, u32[]{:S(2)}) copy-start(f32[128,2]{0,1:T(2,128)} %param.24) | copy-start | bytes 3076
  227.1 72.0 %copy-start.4 = (s32[256,1]{0,1:T(1,128)S(1)}, s32[256,1]{0,1:T(1,128)}, u32[]{:S(2)}) copy-start(s32[256,1]{0,1:T(1,128)} %copy-done.3) | copy-start | bytes 3076
  227.2 63.9 %reduce-scatter.5.cloned.1.call-start = ((), (), s32[]{:S(2)}) async-start(), calls=%async_computation.9 | async-start | bytes 2654208 | tf_op jit(solution)/shard_map/reduce_scatter | solution.py:68
  291.1 14.9 %all-to-all-start.3 = ((bf16[16,24,384]{2,1,0:T(8,128)(2,1)}), bf16[16,24,384]{2,1,0:T(8,128)(2,1)}, u32[]{:S(2)}, u32[]{:S(2)}) async-start(bf16[16,24,384]{2,1,0:T(8,128)(2,1)} %bitcast.199), calls=%async_computation.5 | async-start | bytes 589824 | tf_op jit(solution)/shard_map/all_to_all | solution.py:206
Sparse Core Ops, SparseCore 0:
  9.7 76.6 all-gather.5
  175.7 37.1 all-gather.7
  227.3 16.5 reduce-scatter.2
  246.3 44.7 reduce-scatter.4
where the time goes:
time: 321 us; the launch traced here: 320 us
  waiting for transfers between devices  146 us (45%)
  blocking collectives  61.2 us (19%)
  local copies, waits for them, and re-layouts  32.1 us (10%)
  other arithmetic  26.2 us (8%)
  starting transfers between devices  20.2 us (6%)
  matrix products  19.8 us (6%)
  between operations  15.3 us (5%)
    reduce_scatter x1, waiting for transfers between devices, summed_rows(): return lax.psum_scatter(tiles, chips, scatter_dimension=0, tiled=True)[0]  47.2 us
    all_gather x1, waiting for transfers between devices, shards(): lax.all_gather(lax.all_to_all(picked_rows.reshape(experts, capacity, moe_...  37.1 us
    all_gather x3, blocking collectives, carried_in(): lax.all_gather(part.astype(kind), axis)  36.6 us
    all_to_all x1, waiting for transfers between devices, sum_at_owner(): tiles = lax.all_to_all(cut_along(x, dim, peers), axis, 0, 0, tiled=True)  21.7 us
    reduce_scatter x1, waiting for transfers between devices, summed_rows(): tiles = lax.psum_scatter(tiles, core, scatter_dimension=0, tiled=True)  16.7 us
    all_to_all x1, blocking collectives, shards(): lax.all_to_all(picked_rows.reshape(experts, capacity, moe_input.shape[1])...  14.6 us
    all_gather x1, waiting for transfers between devices, shards(): lax.all_gather(out_weight, CTX, axis=1, tiled=True)  10.6 us
    unnamed x1, blocking collectives  9.94 us
  transfers between devices with their start and end apart: 7, of which 7 were waited for; matrix products, arithmetic and copies ran while one was open for 12% of the time, Pallas kernels for 0%

commit v1 on v0

--- a/solution.py
+++ b/solution.py
@@ -182,17 +182,25 @@
     picked_rows = jnp.where(
         occupied[:, None], moe_input[source_row], jnp.zeros((), moe_input.dtype)
     )
-    arrived = lax.all_gather(
+    arrived = jnp.concatenate(
         lax.all_to_all(
-            picked_rows.reshape(experts, capacity, moe_input.shape[1]),
-            CTX,
-            split_axis=0,
-            concat_axis=0,
-            tiled=True,
+            jnp.stack(
+                [
+                    lax.all_to_all(
+                        picked_rows.reshape(experts, capacity, moe_input.shape[1]),
+                        CTX,
+                        split_axis=0,
+                        concat_axis=0,
+                        tiled=True,
+                    )
+                ]
+                * lax.axis_size(TP)
+            ),
+            TP,
+            0,
+            0,
         ),
-        TP,
         axis=2,
-        tiled=True,
     )
     flat_in = arrived.reshape(-1, arrived.shape[2])
     gate_pre = jnp.dot(flat_in, gate_weight[0], preferred_element_type=jnp.float32)

time: 321 us -> 391 us (1.22)
  blocking collectives: 61.2 us -> 170 us
  waiting for transfers between devices: 146 us -> 105 us
  local copies, waits for them, and re-layouts: 32.1 us -> 37.3 us
    all_to_all x0 -> x1, blocking collectives: none -> 108 us  [shards(): lax.all_to_all(jnp.stack([lax.all_to_all(picked_rows.reshape(experts, cap...]
    all_gather x1 -> x0, waiting for transfers between devices: 37.1 us -> none  [shards(): lax.all_gather(lax.all_to_all(picked_rows.reshape(experts, capacity, moe_...]
  transfers between devices with their start and end apart: 7 -> 6, of which waited for: 7 -> 6; matrix products, arithmetic and copies ran while one was open for 12% -> 10% of each run, Pallas kernels for 0% -> 0%
where the time goes in v1:
time: 391 us; the launch traced here: 390 us
  blocking collectives  170 us (43%)
  waiting for transfers between devices  105 us (27%)
  local copies, waits for them, and re-layouts  37.3 us (10%)
  other arithmetic  26.2 us (7%)
  starting transfers between devices  19.9 us (5%)
  matrix products  16.2 us (4%)
  between operations  15.3 us (4%)
    all_to_all x1, blocking collectives, shards(): lax.all_to_all(jnp.stack([lax.all_to_all(picked_rows.reshape(experts, cap...  108 us
    reduce_scatter x1, waiting for transfers between devices, summed_rows(): return lax.psum_scatter(tiles, chips, scatter_dimension=0, tiled=True)[0]  47.1 us
    all_gather x3, blocking collectives, carried_in(): lax.all_gather(part.astype(kind), axis)  36.6 us
    all_to_all x1, waiting for transfers between devices, sum_at_owner(): tiles = lax.all_to_all(cut_along(x, dim, peers), axis, 0, 0, tiled=True)  21.7 us
    all_to_all x1, blocking collectives, shards(): lax.all_to_all(picked_rows.reshape(experts, capacity, moe_input.shape[1])...  14.5 us
    reduce_scatter x1, waiting for transfers between devices, summed_rows(): tiles = lax.psum_scatter(tiles, core, scatter_dimension=0, tiled=True)  13.7 us
    all_gather x1, waiting for transfers between devices, shards(): lax.all_gather(out_weight, CTX, axis=1, tiled=True)  10.6 us
    unnamed x1, blocking collectives  9.94 us
  transfers between devices with their start and end apart: 6, of which 6 were waited for; matrix products, arithmetic and copies ran while one was open for 10% of the time, Pallas kernels for 0%

profile of v1, /device:TPU:2, one launch (start us, length us, event | category | flops | bytes accessed | tf_op | source)
XLA Modules:
  0.0 389.8 jit_solution(14148434395901354257)
XLA Ops:
  6.5 0.7 all-gather.5.cloned.1.call-update
  7.3 1.1 reduce-window.19
  8.4 1.3 fusion.98
  12.2 1.3 dynamic-slice
  14.2 0.7 fusion.97
  15.1 9.9 %all-reduce = bf16[16]{0:T(256)(128)(2,1)S(1)} all-reduce(bf16[16]{0:T(256)(128)(2,1)S(1)} %dynamic-update-slice), channel_id=2, replica_groups=mesh['ctx_0'=4,'ctx_1'=4,'tp_0'=8,'tp_1'=2] {'ctx_1'}, use_global_device_ids=true, to_apply=%add | all-reduce | flops 16 | bytes 64
  25.7 8.6 %all-gather.2 = bf16[4,1,4]{2,1,0:T(2,128)(2,1)S(1)} all-gather(bf16[1,1,4]{2,1,0:T(2,128)(2,1)S(1)} %bitcast.212), channel_id=1, replica_groups=mesh['ctx_0'=4,'ctx_1'=4,'tp_0'=8,'tp_1'=2] {'ctx_0'}, dimensions={0}, use_global_device_ids=true | all-gather | bytes 40 | tf_op jit(solution)/shard_map/all_gather | solution.py:26
  34.3 1.7 copy.95
  36.6 1.3 broadcast_compare_fusion
  38.6 1.2 convolution_convert_fusion.2
  39.8 12.2 %all-gather.1 = bf16[16,128,128]{2,1,0:T(8,128)(2,1)S(1)} all-gather(bf16[4,128,128]{2,1,0:T(8,128)(2,1)S(1)} %convolution_convert_fusion.2), channel_id=3, replica_groups=mesh['ctx_0'=4,'ctx_1'=4,'tp_0'=8,'tp_1'=2] {'ctx_1'}, dimensions={0}, use_global_device_ids=true | all-gather | bytes 655360 | tf_op jit(solution)/shard_map/all_gather | solution.py:26
  52.1 0.7 copy-done.1
  53.0 15.7 %all_gather.28 = bf16[4,4,128,128]{3,2,1,0:T(8,128)(2,1)} all-gather(bf16[1,4,128,128]{3,2,1,0:T(8,128)(2,1)S(1)} %fusion.28), channel_id=1, replica_groups=mesh['ctx_0'=4,'ctx_1'=4,'tp_0'=8,'tp_1'=2] {'ctx_0'}, dimensions={0}, use_global_device_ids=true | all-gather | bytes 655360 | tf_op jit(solution)/shard_map/all_gather | solution.py:26
  69.9 0.8 fusion.88
  70.7 2.1 convolution_bitcast_fusion.1
  72.9 2.1 multiply_reduce_fusion.1
  75.1 0.8 fusion.37
  75.8 10.6 %all-gather.5.cloned.1.call-done = bf16[512,6144]{1,0:T(8,128)(2,1)} async-done(((bf16[512,384]{1,0:T(8,128)(2,1)}), bf16[512,6144]{1,0:T(8,128)(2,1)}) %all-gather.5.cloned.1.call-update) | async-done | bytes 6291472 | tf_op jit(solution)/shard_map/all_gather | solution.py:160
  86.4 3.9 convolution_convert_fusion.1
  90.4 1.4 copy.125
  91.7 7.7 %all-to-all-start = ((bf16[16,128,384]{2,1,0:T(8,128)(2,1)}), bf16[16,128,384]{2,1,0:T(8,128)(2,1)}, u32[]{:S(2)}, u32[]{:S(2)}) async-start(bf16[16,128,384]{2,1,0:T(8,128)(2,1)} %bitcast.199), calls=%async_computation | async-start | bytes 3145728 | tf_op jit(solution)/shard_map/all_to_all | solution.py:49
  99.5 0.7 copy.86
  100.2 1.0 eq.77
  101.2 1.6 eq.73
  103.4 1.3 reduce-window.20
  104.7 0.7 slice_reduce_fusion
  105.4 1.2 reduce-window.21
  106.6 1.2 slice.75
  107.8 1.3 broadcast_multiply_fusion.1
  109.1 1.4 copy.85
  110.5 1.6 mul.332
  112.6 0.8 fusion.91
  113.4 0.7 compare_select_fusion
  114.1 1.6 scatter_custom_fusion.1
  115.7 21.7 %all-to-all-done = bf16[16,128,384]{2,1,0:T(8,128)(2,1)} async-done(((bf16[16,128,384]{2,1,0:T(8,128)(2,1)}), bf16[16,128,384]{2,1,0:T(8,128)(2,1)}, u32[]{:S(2)}, u32[]{:S(2)}) %all-to-all-start) | async-done | bytes 1572896 | tf_op jit(solution)/shard_map/all_to_all | solution.py:49
  137.4 1.6 convert_reduce_fusion
  139.0 1.6 fusion.47
  141.2 4.8 %all-to-all-start.1 = ((f32[16,1,128]{2,1,0:T(1,128)}), f32[16,1,128]{2,1,0:T(1,128)S(1)}, u32[]{:S(2)}, u32[]{:S(2)}) async-start(f32[16,1,128]{2,1,0:T(1,128)} %broadcast_in_dim.65), calls=%async_computation.1 | async-start | bytes 16384 | tf_op jit(solution)/shard_map/all_to_all | solution.py:55
  146.1 2.1 scatter_custom_fusion
  148.2 0.7 broadcast_in_dim.63
  148.9 4.7 %all-to-all-done.1 = f32[16,1,128]{2,1,0:T(1,128)S(1)} async-done(((f32[16,1,128]{2,1,0:T(1,128)}), f32[16,1,128]{2,1,0:T(1,128)S(1)}, u32[]{:S(2)}, u32[]{:S(2)}) %all-to-all-start.1) | async-done | bytes 8224 | tf_op jit(solution)/shard_map/all_to_all | solution.py:55
  154.2 0.7 add_rsqrt_fusion.1
  154.9 1.6 fusion.49
  156.5 3.3 gather_fusion
  159.9 1.1 broadcast_select_fusion
  160.9 14.5 %all_to_all.26 = bf16[16,24,384]{2,1,0:T(8,128)(2,1)S(1)} all-to-all(bf16[16,24,384]{2,1,0:T(8,128)(2,1)S(1)} %broadcast_select_fusion), channel_id=1, replica_groups=mesh['ctx_0'=4,'ctx_1'=4,'tp_0'=8,'tp_1'=2] {'ctx_0','ctx_1'}, dimensions={0} | all-to-all | bytes 589824 | tf_op jit(solution)/shard_map/all_to_all | solution.py:189
  175.5 0.7 stack.2
  176.2 108.5 %all_to_all.27 = bf16[16,16,24,384]{3,2,1,0:T(8,128)(2,1)S(1)} all-to-all(bf16[16,16,24,384]{3,2,1,0:T(8,128)(2,1)S(1)} %stack.2), channel_id=1, replica_groups=mesh['ctx_0'=4,'ctx_1'=4,'tp_0'=8,'tp_1'=2] {'tp_0','tp_1'}, dimensions={0} | all-to-all | bytes 9437184 | tf_op jit(solution)/shard_map/all_to_all | solution.py:186
  284.6 2.8 copy.90
  287.4 1.6 copy.101
  289.4 2.0 fusion.3
  291.5 2.0 fusion.8
  293.5 2.9 convolution_convert_fusion
  296.4 0.7 copy.124
  297.1 2.7 copy.92
  299.8 13.7 %reduce-scatter.3.cloned.1.call-done = bf16[8,384,384]{2,1,0:T(8,128)(2,1)} async-done(((bf16[16,384,384]{2,1,0:T(8,128)(2,1)}), bf16[8,384,384]{2,1,0:T(8,128)(2,1)}) %reduce-scatter.3.cloned.1.call-update) | async-done | bytes 2359312 | tf_op jit(solution)/shard_map/reduce_scatter | solution.py:67
  313.5 47.1 %reduce-scatter.5.cloned.1.call-done = bf16[1,384,384]{2,1,0:T(8,128)(2,1)} async-done(((bf16[8,384,384]{2,1,0:T(8,128)(2,1)}), bf16[1,384,384]{2,1,0:T(8,128)(2,1)}) %reduce-scatter.5.cloned.1.call-update) | async-done | bytes 294928 | tf_op jit(solution)/shard_map/reduce_scatter | solution.py:68
  360.6 7.3 %all-to-all-start.4 = ((bf16[16,24,384]{2,1,0:T(8,128)(2,1)}), bf16[16,24,384]{2,1,0:T(8,128)(2,1)}, u32[]{:S(2)}, u32[]{:S(2)}) async-start(bf16[16,24,384]{2,1,0:T(8,128)(2,1)} %bitcast.206), calls=%async_computation.6 | async-start | bytes 589824 | tf_op jit(solution)/shard_map/all_to_all | solution.py:214
  367.9 0.7 copy.93
  368.7 6.9 %all-to-all-done.4 = bf16[16,24,384]{2,1,0:T(8,128)(2,1)} async-done(((bf16[16,24,384]{2,1,0:T(8,128)(2,1)}), bf16[16,24,384]{2,1,0:T(8,128)(2,1)}, u32[]{:S(2)}, u32[]{:S(2)}) %all-to-all-start.4) | async-done | bytes 294944 | tf_op jit(solution)/shard_map/all_to_all | solution.py:214
  375.5 2.8 gather_fusion.1
  378.3 1.9 reshape.437
  380.2 1.5 multiply_reduce_fusion
  381.7 1.6 fusion.50
  (60 shorter events, 7.8 us)
Async XLA Ops:
  6.5 286.9 %copy-start = (bf16[1,288,6144]{2,1,0:T(8,128)(2,1)S(1)}, bf16[1,288,6144]{2,1,0:T(8,128)(2,1)}, u32[]{:S(2)}) copy-start(bf16[1,288,6144]{2,1,0:T(8,128)(2,1)} %param.27) | copy-start | bytes 10616836
  6.5 79.9 %all-gather.5.cloned.1.call-start = ((), (), s32[]{:S(2)}) async-start(), calls=%async_computation.7 | async-start | bytes 6684672 | tf_op jit(solution)/shard_map/all_gather | solution.py:160
  9.8 1.2 copy-start.13
  9.8 0.6 copy-start.10
  14.9 54.4 %copy-start.11 = (f32[4]{0:T(128)}, f32[4]{0:T(128)S(1)}, u32[]{:S(2)}) copy-start(f32[4]{0:T(128)S(1)} %get-tuple-element.10) | copy-start | bytes 52
  25.7 43.6 %copy-start.9 = (f32[4]{0:T(128)}, f32[4]{0:T(128)S(1)}, u32[]{:S(2)}) copy-start(f32[4]{0:T(128)S(1)} %get-tuple-element.16) | copy-start | bytes 52
  52.0 0.8 copy-start.1
  52.1 17.8 %copy-start.6 = (f32[4]{0:T(128)}, f32[4]{0:T(128)S(1)}, u32[]{:S(2)}) copy-start(f32[4]{0:T(128)S(1)} %get-tuple-element.21) | copy-start | bytes 52
  52.1 17.8 %copy-start.7 = (f32[4]{0:T(128)}, f32[4]{0:T(128)S(1)}, u32[]{:S(2)}) copy-start(f32[4]{0:T(128)S(1)} %get-tuple-element.22) | copy-start | bytes 52
  52.1 17.8 %copy-start.8 = (f32[4]{0:T(128)}, f32[4]{0:T(128)S(1)}, u32[]{:S(2)}) copy-start(f32[4]{0:T(128)S(1)} %get-tuple-element.23) | copy-start | bytes 52
  72.9 2.2 copy-start.5
  90.3 9.2 %copy-start.2 = (s32[128,2]{0,1:T(2,128)S(1)}, s32[128,2]{0,1:T(2,128)}, u32[]{:S(2)}) copy-start(s32[128,2]{0,1:T(2,128)} %param.23) | copy-start | bytes 3076
  91.7 45.7 %all-to-all-start = ((bf16[16,128,384]{2,1,0:T(8,128)(2,1)}), bf16[16,128,384]{2,1,0:T(8,128)(2,1)}, u32[]{:S(2)}, u32[]{:S(2)}) async-start(bf16[16,128,384]{2,1,0:T(8,128)(2,1)} %bitcast.199), calls=%async_computation | async-start | bytes 3145728 | tf_op jit(solution)/shard_map/all_to_all | solution.py:49
  114.1 27.1 %copy-start.3 = (s32[256,1]{0,1:T(1,128)}, s32[256,1]{0,1:T(1,128)S(1)}, u32[]{:S(2)}) copy-start(s32[256,1]{0,1:T(1,128)S(1)} %compare_select_fusion) | copy-start | bytes 3076
  141.2 12.4 %all-to-all-start.1 = ((f32[16,1,128]{2,1,0:T(1,128)}), f32[16,1,128]{2,1,0:T(1,128)S(1)}, u32[]{:S(2)}, u32[]{:S(2)}) async-start(f32[16,1,128]{2,1,0:T(1,128)} %broadcast_in_dim.65), calls=%async_computation.1 | async-start | bytes 16384 | tf_op jit(solution)/shard_map/all_to_all | solution.py:55
  146.0 167.5 %reduce-scatter.3.cloned.1.call-start = ((), (), s32[]{:S(2)}) async-start(), calls=%async_computation.8 | async-start | bytes 7077888 | tf_op jit(solution)/shard_map/reduce_scatter | solution.py:67
  287.4 2.0 copy-start.14
  289.4 2.0 copy-start.15
  299.8 68.1 %copy-start.12 = (f32[128,2]{0,1:T(2,128)S(1)}, f32[128,2]{0,1:T(2,128)}, u32[]{:S(2)}) copy-start(f32[128,2]{0,1:T(2,128)} %param.24) | copy-start | bytes 3076
  299.8 68.9 %copy-start.4 = (s32[256,1]{0,1:T(1,128)S(1)}, s32[256,1]{0,1:T(1,128)}, u32[]{:S(2)}) copy-start(s32[256,1]{0,1:T(1,128)} %copy-done.3) | copy-start | bytes 3076
  299.8 60.8 %reduce-scatter.5.cloned.1.call-start = ((), (), s32[]{:S(2)}) async-start(), calls=%async_computation.9 | async-start | bytes 2654208 | tf_op jit(solution)/shard_map/reduce_scatter | solution.py:68
  360.6 14.9 %all-to-all-start.4 = ((bf16[16,24,384]{2,1,0:T(8,128)(2,1)}), bf16[16,24,384]{2,1,0:T(8,128)(2,1)}, u32[]{:S(2)}, u32[]{:S(2)}) async-start(bf16[16,24,384]{2,1,0:T(8,128)(2,1)} %bitcast.206), calls=%async_computation.6 | async-start | bytes 589824 | tf_op jit(solution)/shard_map/all_to_all | solution.py:214
Sparse Core Ops, SparseCore 0:
  9.7 76.6 all-gather.4
  299.9 13.5 reduce-scatter.2
  316.1 44.4 reduce-scatter.4
